TPU v7x, 256 devices: a whole 4x4x8 slice. The times are simulated.
256 devices in a mesh: space: 32 (over x, y, core), tm: 8 (over z).
Axes of the slice: x: 4, y: 4, z: 8, core: 2. Of those that a mesh axis runs over, the one named last changes fastest.
Arguments:
- velocity: bfloat16 [256, 2, 512, 1024], P('tm', None, 'space'), may hold values from -8.4 to 8.4
Outputs:
- vorticity: bfloat16 [256, 512, 1024], P('tm', 'space')
- modes: float32 [32, 512, 1024], P('tm', 'space')
All inputs are finite; a program needn't handle non-finite values.
Results may differ from a plain program's by a relative error of at most 0.003.
Values may be sent and summed in bfloat16 or wider, within the bound.
A program may use at most 64 MiB of HBM per device.

v0:
```python
import jax
import jax.numpy as jnp
from jax import lax
from jax.sharding import PartitionSpec as P

RANK = 32
HIGH = lax.Precision.HIGHEST


def halo_rows(block, width):
    count = lax.axis_size("space")
    forward = [(i, (i + 1) % count) for i in range(count)]
    backward = [(target, source) for source, target in forward]
    rows = block.shape[1]
    low = lax.ppermute(block[:, rows - width :], "space", forward)
    high = lax.ppermute(block[:, :width], "space", backward)
    return jnp.concatenate([low, block, high], axis=1)


def spanwise(field):
    ahead = jnp.roll(field, -1, 2)
    behind = jnp.roll(field, 1, 2)
    ahead_two = jnp.roll(field, -2, 2)
    behind_two = jnp.roll(field, 2, 2)
    return (8.0 * (ahead - behind) - (ahead_two - behind_two)) / 12.0


def merge_small(gram):
    coeffs = gram[:, :, :RANK] + gram[:, :, RANK:]
    diagonal = jnp.diagonal(gram, axis1=1, axis2=2)
    scales = jnp.sqrt(diagonal[:, :RANK] + diagonal[:, RANK:])
    half = jnp.einsum("nab,nbc->nac", gram, coeffs, precision=HIGH)
    inner = jnp.einsum("nab,nac->nbc", coeffs, half, precision=HIGH)
    lower = jnp.linalg.cholesky(inner)
    eye = jnp.broadcast_to(jnp.eye(RANK, dtype=jnp.float32), inner.shape)
    lower_inv = lax.linalg.triangular_solve(lower, eye, left_side=True, lower=True)
    factor = jnp.swapaxes(lower_inv, 1, 2) * scales[:, None, :]
    return jnp.einsum("nab,nbc->nac", coeffs, factor, precision=HIGH)


def tree_basis(gram, leaves):
    width = leaves * RANK
    basis = None
    span = 1
    while span < leaves:
        nodes = leaves // (2 * span)
        size = 2 * span * RANK
        sub = jnp.stack(
            [gram[k * size : (k + 1) * size, k * size : (k + 1) * size] for k in range(nodes)]
        )
        if basis is None:
            h = sub
        else:
            b = basis.reshape(nodes, 2, span * RANK, RANK)
            zero = jnp.zeros_like(b[:, 0])
            bd = jnp.concatenate(
                [
                    jnp.concatenate([b[:, 0], zero], axis=2),
                    jnp.concatenate([zero, b[:, 1]], axis=2),
                ],
                axis=1,
            )
            gb = jnp.einsum("nab,nbc->nac", sub, bd, precision=HIGH)
            h = jnp.einsum("nab,nac->nbc", bd, gb, precision=HIGH)
        c = merge_small(h)
        if basis is None:
            basis = c
        else:
            basis = jnp.einsum("nab,nbc->nac", bd, c, precision=HIGH)
        span *= 2
    return basis.reshape(width, RANK)


def local(velocity):
    rows = velocity.shape[2]
    span_v = halo_rows(velocity[:, 1], 2).astype(jnp.float32)
    stream_u = velocity[:, 0].astype(jnp.float32)
    dv_dx = (
        8.0 * (span_v[:, 3 : rows + 3] - span_v[:, 1 : rows + 1])
        - (span_v[:, 4:] - span_v[:, :rows])
    ) / 12.0
    vorticity = (dv_dx - spanwise(stream_u)).astype(jnp.bfloat16)
    blocks = lax.axis_size("tm")
    cells = lax.all_to_all(vorticity, "tm", 2, 0, tiled=True)
    flat = cells.reshape(cells.shape[0], -1)
    gram = jnp.einsum("ax,bx->ab", flat, flat, preferred_element_type=jnp.float32)
    gram = lax.psum(gram, ("space", "tm"))
    basis = tree_basis(gram, blocks)
    part = jnp.einsum("ab,ax->bx", basis, flat.astype(jnp.float32), precision=HIGH).reshape(
        RANK, rows, -1
    )
    modes = lax.all_to_all(part, "tm", 0, 2, tiled=True)
    return (vorticity, modes)


def solution(mesh):
    in_specs = (P("tm", None, "space", None),)
    out_specs = (P("tm", "space", None), P("tm", "space", None))
    return jax.shard_map(local, mesh=mesh, in_specs=in_specs, out_specs=out_specs, check_vma=False)
```

profile of v0, /device:TPU:2, one launch (start us, length us, event | category | flops | bytes accessed | tf_op | source)
XLA Modules:
  0.0 411.2 jit_solution(9131504356403751906)
XLA Ops:
  7.2 1.9 bitcast_convert_fusion
  9.0 0.6 copy.179
  9.7 3.8 collective-permute-start.1
  13.6 0.7 fusion.72
  14.3 0.7 fusion.74
  15.4 0.8 collective-permute-done
  16.4 0.8 copy_convert_fusion
  17.2 2.2 fusion.3
  19.4 5.1 %copy.130 = bf16[32,16,1024]{0,1,2:T(8,128)(2,1)} copy(bf16[32,16,1024]{2,1,0:T(8,128)(2,1)S(1)} %fusion.3) | data formatting | bytes 2097152 | tf_op jit(solution)/shard_map/convert_element_type | solution.py:82
  24.5 7.8 %reshape.157 = bf16[8,2,32768]{2,1,0:T(2,128)(2,1)} reshape(bf16[1024,16,32]{2,1,0:T(8,128)(2,1)} %bitcast.133) | data formatting | bytes 2097152
  32.4 8.5 %all-to-all-start = ((bf16[8,2,32768]{2,1,0:T(2,128)(2,1)}), bf16[8,2,32768]{2,1,0:T(2,128)(2,1)S(1)}, u32[]{:S(2)}, u32[]{:S(2)}) async-start(bf16[8,2,32768]{2,1,0:T(2,128)(2,1)} %reshape.157), calls=%async_computation | async-start | bytes 2097152 | tf_op jit(solution)/shard_map/all_to_all | solution.py:84
  41.1 28.5 %all-to-all-done = bf16[8,2,32768]{2,1,0:T(2,128)(2,1)S(1)} async-done(((bf16[8,2,32768]{2,1,0:T(2,128)(2,1)}), bf16[8,2,32768]{2,1,0:T(2,128)(2,1)S(1)}, u32[]{:S(2)}, u32[]{:S(2)}) %all-to-all-start) | async-done | bytes 1048608 | tf_op jit(solution)/shard_map/all_to_all | solution.py:84
  69.6 4.5 %reshape.158 = bf16[1024,16,32]{2,1,0:T(8,128)(2,1)} reshape(bf16[8,2,32768]{2,1,0:T(2,128)(2,1)S(1)} %all-to-all-done) | data formatting | bytes 2097152
  74.1 5.4 %copy.131 = bf16[32,16,8,128]{3,1,0,2:T(8,128)(2,1)S(1)} copy(bf16[32,16,8,128]{0,1,3,2:T(8,128)(2,1)} %bitcast.132) | data formatting | bytes 2097152 | tf_op jit(solution)/shard_map/all_to_all | solution.py:84
  79.5 1.2 fusion.10
  80.7 0.7 copy.133
  81.4 0.3 copy.178
  81.7 0.5 copy.152
  82.2 244.6 %all-reduce.6.cloned.1.call-done = f32[256,256]{0,1:T(8,128)} async-done(((f32[256,256]{0,1:T(8,128)}), f32[256,256]{0,1:T(8,128)}) %all-reduce.6.cloned.1.call-update) | async-done | bytes 262160 | tf_op jit(solution)/shard_map/psum | solution.py:87
  326.8 0.9 slice_bitcast_fusion.7
  327.8 1.9 copy.137
  329.7 0.9 fusion.70
  330.6 1.5 gather_fusion
  332.0 0.8 copy.138
  332.9 1.1 fusion.69
  334.1 11.7 %custom-call.21 = f32[4,32,32]{2,1,0:T(8,128)S(1)} custom-call(f32[4,32,32]{2,1,0:T(8,128)S(1)} %fusion.19), custom_call_target="Cholesky" | custom-call | tf_op jit(solution)/shard_map/jit(cholesky)/cholesky | solution.py:34
  346.1 9.8 %custom-call.22 = f32[4,1,32,32]{2,3,1,0:T(8,128)S(1)} custom-call(f32[4,1,32,32]{3,2,1,0:T(8,128)S(1)} %select_bitcast_fusion), custom_call_target="InvertDiagBlocksLowerTriangular" | custom-call | tf_op jit(solution)/shard_map/triangular_solve | solution.py:36
  355.9 0.9 convolution_multiply_fusion
  356.9 0.3 fusion.68
  357.2 0.3 fusion.13
  357.5 0.3 fusion.39
  357.8 1.9 copy.147
  359.7 0.8 fusion.67
  360.5 1.5 gather_fusion.1
  362.0 0.8 copy.148
  362.9 0.9 fusion.66
  363.9 5.9 %custom-call.23 = f32[2,32,32]{2,1,0:T(8,128)S(1)} custom-call(f32[2,32,32]{2,1,0:T(8,128)S(1)} %fusion.32), custom_call_target="Cholesky" | custom-call | tf_op jit(solution)/shard_map/jit(cholesky)/cholesky | solution.py:34
  370.0 4.9 %custom-call.24 = f32[2,1,32,32]{2,3,1,0:T(8,128)S(1)} custom-call(f32[2,1,32,32]{3,2,1,0:T(8,128)S(1)} %select_bitcast_fusion.1), custom_call_target="InvertDiagBlocksLowerTriangular" | custom-call | tf_op jit(solution)/shard_map/triangular_solve | solution.py:36
  375.0 0.9 convolution_multiply_fusion.1
  376.4 0.3 fusion.23
  376.9 0.8 gather_fusion.2
  378.1 2.9 custom-call.25
  381.0 0.6 compare_reduce_fusion
  381.7 0.7 fusion.34
  382.3 2.4 custom-call.26
  385.4 1.0 fusion.76
  386.6 17.1 %all_to_all.33 = f32[32,16,128]{2,1,0:T(8,128)S(1)} all-to-all(f32[32,16,128]{2,1,0:T(8,128)S(1)} %copy.153), channel_id=1, replica_groups=mesh['space'=32,'tm'=8] {'tm'}, dimensions={0} | all-to-all | bytes 524288 | tf_op jit(solution)/shard_map/all_to_all | solution.py:92
  403.7 0.7 copy.180
  (45 shorter events, 3.5 us)
Async XLA Ops:
  9.6 6.6 %collective-permute-start = (bf16[32,2,1024]{2,0,1:T(8,128)(2,1)S(1)}, bf16[32,2,1024]{2,0,1:T(8,128)(2,1)S(1)}, u32[]{:S(2)}, u32[]{:S(2)}) collective-permute-start(bf16[32,2,1024]{2,0,1:T(8,128)(2,1)S(1)} %get-tuple-element.18), channel_id=1, source_target_pairs={{0,8},{8,16},{16,24},{24,32},{32,40},{40,48},{48,56},{56,64},{64,7... | collective-permute-start | bytes 393224 | tf_op jit(solution)/shard_map/ppermute | solution.py:15
  9.7 6.5 %collective-permute-start.1 = (bf16[32,2,1024]{2,0,1:T(8,128)(2,1)S(1)}, bf16[32,2,1024]{2,0,1:T(8,128)(2,1)S(1)}, u32[]{:S(2)}, u32[]{:S(2)}) collective-permute-start(bf16[32,2,1024]{2,0,1:T(8,128)(2,1)S(1)} %get-tuple-element.19), channel_id=1, source_target_pairs={{8,0},{16,8},{24,16},{32,24},{40,32},{48,40},{56,48},{64,56},{72,6... | collective-permute-start | bytes 393224 | tf_op jit(solution)/shard_map/ppermute | solution.py:16
  19.4 5.1 %copy-start = (bf16[32,16,1024]{2,1,0:T(8,128)(2,1)}, bf16[32,16,1024]{2,1,0:T(8,128)(2,1)S(1)}, u32[]{:S(2)}) copy-start(bf16[32,16,1024]{2,1,0:T(8,128)(2,1)S(1)} %fusion.3) | copy-start | bytes 3145732
  32.4 37.2 %all-to-all-start = ((bf16[8,2,32768]{2,1,0:T(2,128)(2,1)}), bf16[8,2,32768]{2,1,0:T(2,128)(2,1)S(1)}, u32[]{:S(2)}, u32[]{:S(2)}) async-start(bf16[8,2,32768]{2,1,0:T(2,128)(2,1)} %reshape.157), calls=%async_computation | async-start | bytes 2097152 | tf_op jit(solution)/shard_map/all_to_all | solution.py:84
  40.8 286.0 %all-reduce.6.cloned.1.call-start = ((), (), s32[]{:S(2)}) async-start(), calls=%async_computation.2 | async-start | bytes 524288 | tf_op jit(solution)/shard_map/psum | solution.py:87
  327.7 29.5 %copy-start.1 = (f32[256,256]{0,1:T(8,128)S(1)}, f32[256,256]{0,1:T(8,128)}, u32[]{:S(2)}) copy-start(f32[256,256]{0,1:T(8,128)} %all-reduce.6.cloned.1.call-done) | copy-start | bytes 786436
Sparse Core Ops, SparseCore 0:
  80.8 245.9 all-reduce.5
where the time goes:
time: 412 us; the launch traced here: 411 us
  waiting for transfers between devices  274 us (67%)
  other arithmetic  44.8 us (11%)
  local copies, waits for them, and re-layouts  37.9 us (9%)
  blocking collectives  17.1 us (4%)
  between operations  14.4 us (3%)
  starting transfers between devices  12.6 us (3%)
  matrix products  10.4 us (3%)
    psum x1, waiting for transfers between devices, local(): gram = lax.psum(gram, ('space', 'tm'))  245 us
    all_to_all x1, waiting for transfers between devices, local(): cells = lax.all_to_all(vorticity, 'tm', 2, 0, tiled=True)  28.5 us
    another operation x9, other arithmetic, merge_small(): lower = jnp.linalg.cholesky(inner)  21.5 us
    another operation x7, other arithmetic, merge_small(): lax.linalg.triangular_solve(lower, eye, left_side=True, lower=True)  18 us
    all_to_all x1, blocking collectives, local(): modes = lax.all_to_all(part, 'tm', 0, 2, tiled=True)  17.1 us
    unnamed x8, local copies, waits for them, and re-layouts  13.2 us
    all_to_all x1, starting transfers between devices, local(): cells = lax.all_to_all(vorticity, 'tm', 2, 0, tiled=True)  8.47 us
  transfers between devices with their start and end apart: 4, of which 3 were waited for; matrix products, arithmetic and copies ran while one was open for 1% of the time, Pallas kernels for 0%

commit v1 on v0

--- a/solution.py
+++ b/solution.py
@@ -84,7 +84,7 @@
     cells = lax.all_to_all(vorticity, "tm", 2, 0, tiled=True)
     flat = cells.reshape(cells.shape[0], -1)
     gram = jnp.einsum("ax,bx->ab", flat, flat, preferred_element_type=jnp.float32)
-    gram = lax.psum(gram, ("space", "tm"))
+    gram = lax.psum(lax.psum(gram, "tm"), "space")
     basis = tree_basis(gram, blocks)
     part = jnp.einsum("ab,ax->bx", basis, flat.astype(jnp.float32), precision=HIGH).reshape(
         RANK, rows, -1

time: 412 us -> 348 us (0.84)
  waiting for transfers between devices: 274 us -> 180 us
  blocking collectives: 17.1 us -> 56 us
  starting transfers between devices: 12.6 us -> 4.18 us
    psum x1 -> x2, waiting for transfers between devices: 245 us -> 179 us  [local(): gram = lax.psum(lax.psum(gram, 'tm'), 'space')]
    all_to_all x0 -> x1, blocking collectives: none -> 37 us  [local(): cells = lax.all_to_all(vorticity, 'tm', 2, 0, tiled=True)]
    all_to_all x1 -> x0, waiting for transfers between devices: 28.5 us -> none  [local(): cells = lax.all_to_all(vorticity, 'tm', 2, 0, tiled=True)]
    all_to_all x1 -> x0, starting transfers between devices: 8.47 us -> none  [local(): cells = lax.all_to_all(vorticity, 'tm', 2, 0, tiled=True)]
where the time goes in v1:
time: 348 us; the launch traced here: 347 us
  waiting for transfers between devices  180 us (52%)
  blocking collectives  56 us (16%)
  other arithmetic  44.8 us (13%)
  local copies, waits for them, and re-layouts  37.1 us (11%)
  between operations  14.4 us (4%)
  matrix products  10.4 us (3%)
  starting transfers between devices  4.18 us (1%)
    psum x2, waiting for transfers between devices, local(): gram = lax.psum(lax.psum(gram, 'tm'), 'space')  179 us
    all_to_all x1, blocking collectives, local(): cells = lax.all_to_all(vorticity, 'tm', 2, 0, tiled=True)  37 us
    another operation x9, other arithmetic, merge_small(): lower = jnp.linalg.cholesky(inner)  21.5 us
    all_to_all x1, blocking collectives, local(): modes = lax.all_to_all(part, 'tm', 0, 2, tiled=True)  19 us
    another operation x7, other arithmetic, merge_small(): lax.linalg.triangular_solve(lower, eye, left_side=True, lower=True)  18 us
    unnamed x8, local copies, waits for them, and re-layouts  12.4 us
  transfers between devices with their start and end apart: 4, of which 3 were waited for; matrix products, arithmetic and copies ran while one was open for 1% of the time, Pallas kernels for 0%

profile of v1, /device:TPU:2, one launch (start us, length us, event | category | flops | bytes accessed | tf_op | source)
XLA Modules:
  0.0 347.1 jit_solution(7667016777236550402)
XLA Ops:
  7.2 1.9 bitcast_convert_fusion
  9.1 0.6 copy.179
  9.8 3.8 %collective-permute-start.1 = (bf16[32,2,1024]{2,0,1:T(8,128)(2,1)S(1)}, bf16[32,2,1024]{2,0,1:T(8,128)(2,1)S(1)}, u32[]{:S(2)}, u32[]{:S(2)}) collective-permute-start(bf16[32,2,1024]{2,0,1:T(8,128)(2,1)S(1)} %get-tuple-element.19), channel_id=1, source_target_pairs={{8,0},{16,8},{24,16},{32,24},{40,32},{48,40},{56,48},{64,56},{72,6... | collective-permute-start | bytes 393224 | tf_op jit(solution)/shard_map/ppermute | solution.py:16
  13.6 0.7 fusion.72
  14.4 0.7 fusion.74
  15.4 0.8 collective-permute-done
  16.4 0.8 copy_convert_fusion
  17.2 2.2 fusion.3
  19.5 5.1 %copy.130 = bf16[32,16,1024]{0,1,2:T(8,128)(2,1)} copy(bf16[32,16,1024]{2,1,0:T(8,128)(2,1)S(1)} %fusion.3) | data formatting | bytes 2097152 | tf_op jit(solution)/shard_map/convert_element_type | solution.py:82
  24.6 7.0 %reshape.157 = bf16[8,2,32768]{2,1,0:T(2,128)(2,1)S(1)} reshape(bf16[1024,16,32]{2,1,0:T(8,128)(2,1)} %bitcast.133) | data formatting | bytes 2097152
  31.6 37.0 %all_to_all.33 = bf16[8,2,32768]{2,1,0:T(2,128)(2,1)S(1)} all-to-all(bf16[8,2,32768]{2,1,0:T(2,128)(2,1)S(1)} %reshape.157), channel_id=1, replica_groups=mesh['space'=32,'tm'=8] {'tm'}, dimensions={0} | all-to-all | bytes 2097152 | tf_op jit(solution)/shard_map/all_to_all | solution.py:84
  68.6 4.5 %reshape.158 = bf16[1024,16,32]{2,1,0:T(8,128)(2,1)} reshape(bf16[8,2,32768]{2,1,0:T(2,128)(2,1)S(1)} %all_to_all.33) | data formatting | bytes 2097152
  73.1 5.4 %copy.131 = bf16[32,16,8,128]{3,1,0,2:T(8,128)(2,1)S(1)} copy(bf16[32,16,8,128]{0,1,3,2:T(8,128)(2,1)} %bitcast.132) | data formatting | bytes 2097152 | tf_op jit(solution)/shard_map/all_to_all | solution.py:84
  78.5 1.2 fusion.10
  80.0 68.0 %all-reduce.7.cloned.1.call-done = f32[256,256]{0,1:T(8,128)} async-done(((f32[256,256]{0,1:T(8,128)}), f32[256,256]{0,1:T(8,128)}) %all-reduce.7.cloned.1.call-update) | async-done | bytes 262160 | tf_op jit(solution)/shard_map/psum | solution.py:87
  148.0 0.7 copy.133
  148.6 0.3 copy.178
  148.9 0.5 copy.152
  149.4 111.4 %all-reduce.9.cloned.1.call-done = f32[256,256]{0,1:T(8,128)} async-done(((f32[256,256]{0,1:T(8,128)}), f32[256,256]{0,1:T(8,128)}) %all-reduce.9.cloned.1.call-update) | async-done | bytes 262160 | tf_op jit(solution)/shard_map/psum | solution.py:87
  260.8 0.9 slice_bitcast_fusion.7
  261.7 1.9 copy.137
  263.7 0.9 fusion.70
  264.5 1.5 gather_fusion
  266.0 0.8 copy.138
  266.9 1.1 fusion.69
  268.1 11.7 %custom-call.21 = f32[4,32,32]{2,1,0:T(8,128)S(1)} custom-call(f32[4,32,32]{2,1,0:T(8,128)S(1)} %fusion.19), custom_call_target="Cholesky" | custom-call | tf_op jit(solution)/shard_map/jit(cholesky)/cholesky | solution.py:34
  280.1 9.8 %custom-call.22 = f32[4,1,32,32]{2,3,1,0:T(8,128)S(1)} custom-call(f32[4,1,32,32]{3,2,1,0:T(8,128)S(1)} %select_bitcast_fusion), custom_call_target="InvertDiagBlocksLowerTriangular" | custom-call | tf_op jit(solution)/shard_map/triangular_solve | solution.py:36
  289.9 0.9 convolution_multiply_fusion
  290.9 0.3 fusion.68
  291.2 0.3 fusion.13
  291.5 0.3 fusion.39
  291.8 1.9 copy.147
  293.7 0.8 fusion.67
  294.5 1.5 gather_fusion.1
  296.0 0.8 copy.148
  296.9 0.9 fusion.66
  297.9 5.9 %custom-call.23 = f32[2,32,32]{2,1,0:T(8,128)S(1)} custom-call(f32[2,32,32]{2,1,0:T(8,128)S(1)} %fusion.32), custom_call_target="Cholesky" | custom-call | tf_op jit(solution)/shard_map/jit(cholesky)/cholesky | solution.py:34
  304.0 4.9 %custom-call.24 = f32[2,1,32,32]{2,3,1,0:T(8,128)S(1)} custom-call(f32[2,1,32,32]{3,2,1,0:T(8,128)S(1)} %select_bitcast_fusion.1), custom_call_target="InvertDiagBlocksLowerTriangular" | custom-call | tf_op jit(solution)/shard_map/triangular_solve | solution.py:36
  308.9 0.9 convolution_multiply_fusion.1
  310.3 0.3 fusion.23
  310.8 0.8 gather_fusion.2
  312.0 2.9 custom-call.25
  315.0 0.6 compare_reduce_fusion
  315.6 0.7 fusion.34
  316.3 2.4 custom-call.26
  319.4 1.0 fusion.76
  320.5 19.0 %all_to_all.34 = f32[32,16,128]{2,1,0:T(8,128)S(1)} all-to-all(f32[32,16,128]{2,1,0:T(8,128)S(1)} %copy.153), channel_id=1, replica_groups=mesh['space'=32,'tm'=8] {'tm'}, dimensions={0} | all-to-all | bytes 524288 | tf_op jit(solution)/shard_map/all_to_all | solution.py:92
  339.5 0.7 copy.180
  (47 shorter events, 3.6 us)
Async XLA Ops:
  7.2 140.8 %all-reduce.7.cloned.1.call-start = ((), (), s32[]{:S(2)}) async-start(), calls=%async_computation.2 | async-start | bytes 524288 | tf_op jit(solution)/shard_map/psum | solution.py:87
  9.7 6.6 %collective-permute-start = (bf16[32,2,1024]{2,0,1:T(8,128)(2,1)S(1)}, bf16[32,2,1024]{2,0,1:T(8,128)(2,1)S(1)}, u32[]{:S(2)}, u32[]{:S(2)}) collective-permute-start(bf16[32,2,1024]{2,0,1:T(8,128)(2,1)S(1)} %get-tuple-element.18), channel_id=1, source_target_pairs={{0,8},{8,16},{16,24},{24,32},{32,40},{40,48},{48,56},{56,64},{64,7... | collective-permute-start | bytes 393224 | tf_op jit(solution)/shard_map/ppermute | solution.py:15
  9.8 6.5 %collective-permute-start.1 = (bf16[32,2,1024]{2,0,1:T(8,128)(2,1)S(1)}, bf16[32,2,1024]{2,0,1:T(8,128)(2,1)S(1)}, u32[]{:S(2)}, u32[]{:S(2)}) collective-permute-start(bf16[32,2,1024]{2,0,1:T(8,128)(2,1)S(1)} %get-tuple-element.19), channel_id=1, source_target_pairs={{8,0},{16,8},{24,16},{32,24},{40,32},{48,40},{56,48},{64,56},{72,6... | collective-permute-start | bytes 393224 | tf_op jit(solution)/shard_map/ppermute | solution.py:16
  19.5 5.1 %copy-start = (bf16[32,16,1024]{2,1,0:T(8,128)(2,1)}, bf16[32,16,1024]{2,1,0:T(8,128)(2,1)S(1)}, u32[]{:S(2)}) copy-start(bf16[32,16,1024]{2,1,0:T(8,128)(2,1)S(1)} %fusion.3) | copy-start | bytes 3145732
  79.7 181.1 %all-reduce.9.cloned.1.call-start = ((), (), s32[]{:S(2)}) async-start(), calls=%async_computation.3 | async-start | bytes 524288 | tf_op jit(solution)/shard_map/psum | solution.py:87
  261.7 29.5 %copy-start.1 = (f32[256,256]{0,1:T(8,128)S(1)}, f32[256,256]{0,1:T(8,128)}, u32[]{:S(2)}) copy-start(f32[256,256]{0,1:T(8,128)} %all-reduce.9.cloned.1.call-done) | copy-start | bytes 786436
Sparse Core Ops, SparseCore 0:
  79.8 68.0 all-reduce.6
  151.5 109.3 all-reduce.8
